TPU v7x, 512 devices: a whole 4x8x8 slice. The times are simulated.
512 devices in a mesh: dp: 8 (over y), seq: 64 (over z, x, core).
Axes of the slice: x: 4, y: 8, z: 8, core: 2. Of those that a mesh axis runs over, the one named last changes fastest.
Arguments:
- queries: bfloat16 [8, 8192, 1536], P('dp', 'seq'), may hold values from -6 to 6
- keys: bfloat16 [8, 8192, 1536], P('dp', 'seq'), may hold values from -6 to 6
- values: bfloat16 [8, 8192, 1536], P('dp', 'seq'), may hold values from -6 to 6
- segment_ids: int32 [8, 8192], P('dp'), may hold values from 0 to 127, never falling along the last dimension, each value on 1 to 128 neighbouring positions
- norm_gain: float32 [1536], replicated, may hold values from 0.25 to 1.75
- conv_kernel: float32 [31, 1536], replicated, may hold values from -1 to 1
- conv_bias: float32 [1536], replicated, may hold values from -3 to 3
- cotangent: bfloat16 [8, 8192, 1536], P('dp', 'seq'), may hold values from -6 to 6
Outputs:
- conv_out: bfloat16 [8, 8192, 1536], P('dp', 'seq')
- query_grad: bfloat16 [8, 8192, 1536], P('dp', 'seq')
- key_grad: bfloat16 [8, 8192, 1536], P('dp', 'seq')
- value_grad: bfloat16 [8, 8192, 1536], P('dp', 'seq')
- gain_grad: float32 [1536], replicated
- kernel_grad: float32 [31, 1536], replicated
- bias_grad: float32 [1536], replicated
Inputs may be any that keep to these rules, and one draw needn't show every extreme that they name: `segment_ids`: within each row, utterance numbers never fall; each utterance holds 1 to 128 frames, and some utterance exactly 128.
All inputs are finite; a program needn't handle non-finite values.
Results may differ from a plain program's by a relative error of at most 0.023.
Values may be sent and summed in bfloat16 or wider, within the bound.
A program may use at most 64 MiB of HBM per device.

v0:
```python
import jax
import jax.numpy as jnp
from jax import lax
from jax.sharding import PartitionSpec as P

HEADS = 24
HEAD_DIM = 64
HEAD_BLOCK = 4
REACH = 1
EPS = 1e-05
NEG = -1e30


def shifted(block, axis, distance):
    devices = range(lax.axis_size(axis))
    route = [(i - distance, i) for i in devices if i - distance in devices]
    return lax.ppermute(block, axis, route)


def with_halo(cells, sides, width):
    for axis, dim in sides:
        count = lax.axis_size(axis)
        ends = count - 1
        head = lax.slice_in_dim(cells, 0, width, axis=dim)
        tail = lax.slice_in_dim(cells, cells.shape[dim] - width, cells.shape[dim], axis=dim)
        cells = jnp.concatenate(
            [
                lax.ppermute(tail, axis, [(i, (i + 1) % count) for i in range(ends)]),
                cells,
                lax.ppermute(head, axis, [((i + 1) % count, i) for i in range(ends)]),
            ],
            axis=dim,
        )
    return cells


def to_groups(tensor, block):
    rows_in, heads_in, dim_in = tensor.shape
    return tensor.reshape(rows_in, heads_in // block, block, dim_in).transpose(1, 0, 2, 3)


def from_groups(tensor):
    groups_in, rows_in, block, dim_in = tensor.shape
    return tensor.transpose(1, 0, 2, 3).reshape(rows_in, groups_in * block * dim_in)


def masked_logits(query_rows, key_rows, same_seg):
    factor = query_rows.shape[-1] ** (-0.5)
    logits = (
        jnp.einsum("qhe,khe->hqk", query_rows, key_rows, preferred_element_type=jnp.float32)
        * factor
    )
    return jnp.where(same_seg[None], logits, NEG)


def forward_block(query_rows, key_rows, value_rows, same_seg):
    logits = masked_logits(query_rows, key_rows, same_seg)
    row_top = jnp.max(logits, -1, keepdims=True)
    exponent = jnp.exp(logits - row_top)
    row_total = jnp.sum(exponent, -1, keepdims=True)
    attn_weights = (exponent / row_total).astype(jnp.bfloat16)
    context = jnp.einsum(
        "hqk,khe->qhe", attn_weights, value_rows, preferred_element_type=jnp.float32
    )
    return (context, (row_top + jnp.log(row_total))[..., 0])


def back_terms(query_rows, key_rows, value_rows, grad_rows, log_total, row_delta, same_seg):
    factor = query_rows.shape[-1] ** (-0.5)
    logits = masked_logits(query_rows, key_rows, same_seg)
    prob_back = jnp.exp(logits - log_total[:, :, None])
    grad_prob = jnp.einsum(
        "qhe,khe->hqk", grad_rows, value_rows, preferred_element_type=jnp.float32
    )
    grad_logit = (prob_back * (grad_prob - row_delta[:, :, None]) * factor).astype(jnp.bfloat16)
    return (prob_back.astype(jnp.bfloat16), grad_logit)


def per_device(queries, keys, values, segment_ids, norm_gain, conv_kernel, conv_bias, cotangent):
    frame_count = queries.shape[1]
    width = queries.shape[2]
    reach_rows = REACH * frame_count
    tap_count = conv_kernel.shape[0]
    half_taps = tap_count // 2
    block = HEAD_BLOCK
    group_count = HEADS // block
    start_row = lax.axis_index("seq") * frame_count
    seg_row = segment_ids[0]
    seg_padded = jnp.pad(seg_row, (reach_rows, reach_rows), constant_values=-1)
    own_seg = lax.dynamic_slice_in_dim(seg_row, start_row, frame_count)
    window_seg = lax.dynamic_slice_in_dim(seg_padded, start_row, frame_count + 2 * reach_rows)
    conv_seg = lax.dynamic_slice_in_dim(
        seg_padded, start_row + reach_rows - half_taps, frame_count + 2 * half_taps
    )
    same_fwd = own_seg[:, None] == window_seg[None, :]
    query_heads = queries[0].reshape(frame_count, HEADS, HEAD_DIM)
    key_value = jnp.stack((keys[0], values[0]), 1)
    lower_parts = []
    upper_parts = []
    hop = 1
    for offset_by in (hop, -hop):
        arrived = shifted(key_value, "seq", offset_by)
        if offset_by > 0:
            lower_parts.insert(0, arrived)
        else:
            upper_parts.append(arrived)
    key_value_wide = jnp.concatenate(lower_parts + [key_value] + upper_parts, 0)
    query_groups = to_groups(query_heads, block)
    key_groups = to_groups(key_value_wide[:, 0].reshape(-1, HEADS, HEAD_DIM), block)
    value_groups = to_groups(key_value_wide[:, 1].reshape(-1, HEADS, HEAD_DIM), block)

    def forward_group(operands):
        return forward_block(operands[0], operands[1], operands[2], same_fwd)

    context_groups, total_groups = lax.map(forward_group, (query_groups, key_groups, value_groups))
    context = from_groups(context_groups).astype(jnp.bfloat16)
    context_f = context.astype(jnp.float32)
    row_mean = jnp.mean(context_f, -1, keepdims=True)
    centred = context_f - row_mean
    inv_std = lax.rsqrt(jnp.mean(centred * centred, -1, keepdims=True) + EPS)
    normed = centred * inv_std
    conv_in = (normed * norm_gain).astype(jnp.bfloat16)
    conv_wide = with_halo(conv_in, (("seq", 0),), half_taps).astype(jnp.float32)
    same_taps = [
        (conv_seg[tap_index : tap_index + frame_count] == own_seg)[:, None]
        for tap_index in range(tap_count)
    ]
    pre_act = jnp.broadcast_to(conv_bias, (frame_count, width))
    for tap_index in range(tap_count):
        pre_act = pre_act + conv_kernel[tap_index] * jnp.where(
            same_taps[tap_index], conv_wide[tap_index : tap_index + frame_count], 0.0
        )
    gate_sig = jax.nn.sigmoid(pre_act)
    conv_out = (pre_act * gate_sig).astype(jnp.bfloat16)
    grad_pre = (
        cotangent[0].astype(jnp.float32) * gate_sig * (1.0 + pre_act * (1.0 - gate_sig))
    ).astype(jnp.bfloat16)
    grad_pre_f = grad_pre.astype(jnp.float32)
    bias_part = jnp.sum(grad_pre_f, 0)
    kernel_rows = []
    for tap_index in range(tap_count):
        kernel_rows.append(
            jnp.sum(
                jnp.where(
                    same_taps[tap_index],
                    conv_wide[tap_index : tap_index + frame_count] * grad_pre_f,
                    0.0,
                ),
                0,
            )
        )
    kernel_part = jnp.stack(kernel_rows, 0)
    grad_wide = with_halo(grad_pre, (("seq", 0),), half_taps).astype(jnp.float32)
    grad_in = jnp.zeros((frame_count, width), jnp.float32)
    for tap_index in range(tap_count):
        mirror = 2 * half_taps - tap_index
        grad_in = grad_in + conv_kernel[tap_index] * jnp.where(
            same_taps[mirror], grad_wide[mirror : mirror + frame_count], 0.0
        )
    gain_part = jnp.sum(grad_in * normed, 0)
    grad_norm = grad_in * norm_gain
    grad_context = (
        (
            grad_norm
            - jnp.mean(grad_norm, -1, keepdims=True)
            - normed * jnp.mean(grad_norm * normed, -1, keepdims=True)
        )
        * inv_std
    ).astype(jnp.bfloat16)
    row_delta = jnp.sum(
        (grad_context.astype(jnp.float32) * context_f).reshape(frame_count, HEADS, HEAD_DIM), -1
    )
    delta_groups = row_delta.T.reshape(group_count, block, frame_count)
    grad_groups = to_groups(grad_context.reshape(frame_count, HEADS, HEAD_DIM), block)

    def backward_group(operands):
        query_rows, key_rows, value_rows, grad_rows, log_total, delta_rows = operands
        prob_low, grad_logit = back_terms(
            query_rows, key_rows, value_rows, grad_rows, log_total, delta_rows, same_fwd
        )
        query_part = jnp.einsum(
            "hqk,khe->qhe", grad_logit, key_rows, preferred_element_type=jnp.float32
        )
        key_part = jnp.einsum(
            "hqk,qhe->khe", grad_logit, query_rows, preferred_element_type=jnp.float32
        )
        value_part = jnp.einsum(
            "hqk,qhe->khe", prob_low, grad_rows, preferred_element_type=jnp.float32
        )
        return (query_part, key_part, value_part)

    query_blocks, key_blocks, value_blocks = lax.map(
        backward_group,
        (query_groups, key_groups, value_groups, grad_groups, total_groups, delta_groups),
    )
    key_value_grad = jnp.stack((from_groups(key_blocks), from_groups(value_blocks)), 1)
    own_grad = key_value_grad[reach_rows : reach_rows + frame_count]
    hop = 1
    for offset_by in (hop, -hop):
        if offset_by > 0:
            moved_piece = key_value_grad[
                (REACH + hop) * frame_count : (REACH + hop + 1) * frame_count
            ]
        else:
            moved_piece = key_value_grad[
                (REACH - hop) * frame_count : (REACH - hop + 1) * frame_count
            ]
        own_grad = own_grad + shifted(moved_piece.astype(jnp.bfloat16), "seq", offset_by).astype(
            moved_piece.dtype
        )
    key_grad = own_grad[:, 0]
    value_grad = own_grad[:, 1]
    query_grad = from_groups(query_blocks)
    gain_sum, kernel_sum, bias_sum = lax.psum((gain_part, kernel_part, bias_part), ("dp", "seq"))
    norm_factor = (lax.axis_size("dp") * lax.axis_size("seq") * frame_count) ** (-0.5)
    return (
        conv_out[None],
        query_grad.astype(jnp.bfloat16)[None],
        key_grad.astype(jnp.bfloat16)[None],
        value_grad.astype(jnp.bfloat16)[None],
        gain_sum * norm_factor,
        kernel_sum * norm_factor,
        bias_sum * norm_factor,
    )


def solution(mesh):
    placed = (
        P("dp", "seq", None),
        P("dp", "seq", None),
        P("dp", "seq", None),
        P("dp", None),
        P(),
        P(),
        P(),
        P("dp", "seq", None),
    )
    return jax.shard_map(
        per_device,
        mesh=mesh,
        in_specs=placed,
        out_specs=(
            P("dp", "seq", None),
            P("dp", "seq", None),
            P("dp", "seq", None),
            P("dp", "seq", None),
            P(),
            P(),
            P(),
        ),
        check_vma=False,
    )
```

profile of v0, /device:TPU:1, one launch (start us, length us, event | category | flops | bytes accessed | tf_op | source)
XLA Modules:
  0.0 418.6 jit_solution(15522786637393165617)
XLA Ops:
  8.5 8.7 %collective-permute-start.1 = (bf16[128,2,1536]{2,0,1:T(8,128)(2,1)S(1)}, bf16[128,2,1536]{2,0,1:T(8,128)(2,1)S(1)}, u32[]{:S(2)}, u32[]{:S(2)}) collective-permute-start(bf16[128,2,1536]{2,0,1:T(8,128)(2,1)S(1)} %pad_maximum_fusion.2), channel_id=1, source_target_pairs={{1,0},{2,1},{3,2},{4,3},{5,4},{6,5},{7,6},{8,7},{9,8},{10,9},{11,1... | collective-permute-start | bytes 2359304 | tf_op jit(solution)/shard_map/ppermute | solution.py:17
  17.3 1.9 collective-permute-start
  19.2 2.5 slice_reduce_fusion.30
  26.3 1.8 collective-permute-done
  30.7 21.4 %while.28 = (s32[]{:T(128)}, bf16[6,128,4,64]{1,3,2,0:T(8,128)(2,1)S(1)}, f32[6,4,128]{2,1,0:T(4,128)}, bf16[6,384,4,64]{1,3,2,0:T(8,128)(2,1)}, bf16[6,128,4,64...) while((s32[]{:T(128)}, ...), condition=%wide.region_3.4_spmd.clone, body=%wide.region_0.3_spmd.clone.sunk | while | flops 51953152 | bytes 3068009 | solution.py:115
  53.9 4.4 %collective-permute-start.2 = (bf16[15,1536]{0,1:T(8,128)(2,1)}, bf16[15,1536]{0,1:T(8,128)(2,1)}, u32[]{:S(2)}, u32[]{:S(2)}) collective-permute-start(bf16[15,1536]{0,1:T(8,128)(2,1)} %get-tuple-element.291), channel_id=1, source_target_pairs={{0,1},{1,2},{2,3},{3,4},{4,5},{5,6},{6,7},{7,8},{8,9},{9,10},{10,1... | collective-permute-start | bytes 138248 | tf_op jit(solution)/shard_map/ppermute | solution.py:28
  58.3 2.1 collective-permute-start.3
  60.4 2.1 slice_reduce_fusion.29
  64.1 3.6 collective-permute-done.3
  69.6 18.6 %fusion.110 = (f32[1536]{0:T(1024)S(1)}, f32[1536]{0:T(1024)S(1)}, f32[1536]{0:T(1024)S(1)}, f32[1536]{0:T(1024)S(1)}, f32[1536]{0:T(1024)S(1)}, /*index=5*/f32[...) fusion(f32[158,1536]{0,1:T(8,128)S(1)} %maximum_convert_fusion,, ...), kind=kLoop, calls=%fused_computation.158 | loop fusion | flops 25741824 | bytes 26208128 | tf_op jit(solution)/shard_map/reduce_sum | solution.py:143
  88.3 4.4 %fusion.112 = (f32[1536]{0:T(1024)S(1)}, f32[1536]{0:T(1024)S(1)}, f32[1536]{0:T(1024)S(1)}, f32[1536]{0:T(1024)S(1)}, f32[1536]{0:T(1024)S(1)}, /*index=5*/f32[...) fusion(bf16[128,1536]{0,1:T(8,128)(2,1)S(1)} %get-tuple-element.272, ...), kind=kLoop, calls=%fused_computation.160 | loop fusion | flops 5491200 | bytes 7527552 | tf_op jit(solution)/shard_map/reduce_sum | solution.py:143
  92.8 3.7 fusion.114
  97.5 1.9 collective-permute-start.4
  99.4 3.4 collective-permute-start.5
  102.8 2.2 fusion.108
  123.5 6.0 %stack.135 = f32[31,1536]{1,0:T(8,128)} concatenate(f32[1,1536]{1,0:T(1,128)} %stack.104, f32[1,1536]{1,0:T(1,128)} %stack.105, f32[1,1536]{1,0:T(1,128)} %stack.106, f32[1,1536]{1,0:T(1,128)} %stack.107, f32[1,1536]{1,0:T(1,128)} %stack.108, f32[1,1536]{1,0:T(1,128)} %stack.109, f32[1,1536]{1,0:T(1,128)} %stack.110, f32[1,1536]{1,0:T(1,128)} %stack.111, f32[1,1536]{1,0:T(1,128)} %stack.112, ...), dimensions={0} | concatenate | bytes 380928 | tf_op jit(solution)/shard_map/stack | solution.py:152
  129.5 1.6 maximum_convert_fusion.1
  131.1 19.2 %fusion.190 = (f32[1536]{0:T(1024)}, f32[128]{0:T(128)S(1)}, f32[128]{0:T(128)S(1)}, f32[128,1536]{0,1:T(8,128)S(1)}) fusion(bf16[6,128,4,64]{1,3,2,0:T(8,128)(2,1)S(1)} %get-tuple-element.104, f32[128]{0:T(128)} %copy-done.59, f32[128]{0:T(128)} %copy-done.57, f32[1536]{0:T(1024)} %param.16, f32[158,1536]{0,1:T(8,128)S(1)} %maximum_convert_fusion.1, ...), kind=kLoop, calls=%fused_computation.277 | loop fusion | flops 19855616 | bytes 25767808 | tf_op jit(solution)/shard_map/reduce_sum | solution.py:160
  152.1 45.3 %while.29 = (s32[]{:T(128)}, bf16[6,128,4,64]{1,3,2,0:T(8,128)(2,1)S(1)}, f32[6,384,4,64]{1,3,2,0:T(8,128)}, f32[6,384,4,64]{1,3,2,0:T(8,128)S(1)}, bf16[6,384,4...) while((s32[]{:T(128)}, ...), condition=%wide.region_10.11_spmd.clone, body=%wide.region_9.10_spmd.clone.sunk | while | flops 127451136 | bytes 5426313 | solution.py:192
  157.9 1.8 fusion.240
  165.4 1.8 fusion.240
  172.9 1.8 fusion.240
  180.5 1.8 fusion.240
  188.0 1.8 fusion.240
  195.6 1.8 fusion.240
  197.4 2.0 fusion.48
  200.9 2.5 collective-permute-start.6
  203.5 2.8 collective-permute-start.7
  207.4 113.5 %all-reduce.1 = (f32[1536]{0:T(1024)S(1)}, f32[1536]{0:T(1024)S(1)}) all-reduce(f32[1536]{0:T(1024)S(1)} %copy-done.39, f32[1536]{0:T(1024)S(1)} %copy-done.38), channel_id=1, replica_groups=mesh['dp'=8,'seq'=64] {'dp','seq'}, use_global_device_ids=true, to_apply=%region_12.13 | all-reduce | flops 3072 | bytes 24576 | tf_op jit(solution)/shard_map/psum | solution.py:214
  322.4 83.9 %all-reduce.4.cloned.1.call-done = f32[31,1536]{1,0:T(8,128)} async-done(((f32[31,1536]{1,0:T(8,128)}), f32[31,1536]{1,0:T(8,128)}) %all-reduce.4.cloned.1.call-update) | async-done | bytes 190480 | tf_op jit(solution)/shard_map/psum | solution.py:214
  406.3 1.6 broadcast_multiply_fusion
  407.9 1.9 fusion.52
  (263 shorter events, 96.0 us)
Async XLA Ops:
  7.2 21.0 %copy-start.2 = (bf16[1,128,1536]{2,1,0:T(8,128)(2,1)S(1)}, bf16[1,128,1536]{2,1,0:T(8,128)(2,1)}, u32[]{:S(2)}) copy-start(bf16[1,128,1536]{2,1,0:T(8,128)(2,1)} %param.14) | copy-start | bytes 1179652
  7.2 21.0 %copy-start.3 = (bf16[1,128,1536]{2,1,0:T(8,128)(2,1)S(1)}, bf16[1,128,1536]{2,1,0:T(8,128)(2,1)}, u32[]{:S(2)}) copy-start(bf16[1,128,1536]{2,1,0:T(8,128)(2,1)} %param.13) | copy-start | bytes 1179652
  7.2 15.3 %copy-start.4 = (bf16[1,128,1536]{2,1,0:T(8,128)(2,1)S(1)}, bf16[1,128,1536]{2,1,0:T(8,128)(2,1)}, u32[]{:S(2)}) copy-start(bf16[1,128,1536]{2,1,0:T(8,128)(2,1)} %param.12) | copy-start | bytes 1179652
  7.2 399.1 %all-reduce.4.cloned.1.call-start = ((), (), s32[]{:S(2)}) async-start(), calls=%async_computation | async-start | bytes 393216 | tf_op jit(solution)/shard_map/psum | solution.py:214
  8.5 17.8 %collective-permute-start.1 = (bf16[128,2,1536]{2,0,1:T(8,128)(2,1)S(1)}, bf16[128,2,1536]{2,0,1:T(8,128)(2,1)S(1)}, u32[]{:S(2)}, u32[]{:S(2)}) collective-permute-start(bf16[128,2,1536]{2,0,1:T(8,128)(2,1)S(1)} %pad_maximum_fusion.2), channel_id=1, source_target_pairs={{1,0},{2,1},{3,2},{4,3},{5,4},{6,5},{7,6},{8,7},{9,8},{10,9},{11,1... | collective-permute-start | bytes 2359304 | tf_op jit(solution)/shard_map/ppermute | solution.py:17
  17.3 10.8 %collective-permute-start = (bf16[128,2,1536]{2,0,1:T(8,128)(2,1)S(1)}, bf16[128,2,1536]{2,0,1:T(8,128)(2,1)S(1)}, u32[]{:S(2)}, u32[]{:S(2)}) collective-permute-start(bf16[128,2,1536]{2,0,1:T(8,128)(2,1)S(1)} %pad_maximum_fusion.2), channel_id=1, source_target_pairs={{0,1},{1,2},{2,3},{3,4},{4,5},{5,6},{6,7},{7,8},{8,9},{9,10},{10,1... | collective-permute-start | bytes 2359304 | tf_op jit(solution)/shard_map/ppermute | solution.py:17
  30.7 21.8 %copy-start.5 = (f32[1536]{0:T(1024)S(1)}, f32[1536]{0:T(1024)}, u32[]{:S(2)}) copy-start(f32[1536]{0:T(1024)} %param.16) | copy-start | bytes 18436
  52.3 8.1 %copy-start.57 = (f32[128]{0:T(128)}, f32[128]{0:T(128)S(1)}, u32[]{:S(2)}) copy-start(f32[128]{0:T(128)S(1)} %broadcast_multiply_fusion.5) | copy-start | bytes 1540
  52.5 7.8 %copy-start.59 = (f32[128]{0:T(128)}, f32[128]{0:T(128)S(1)}, u32[]{:S(2)}) copy-start(f32[128]{0:T(128)S(1)} %add_rsqrt_fusion) | copy-start | bytes 1540
  53.9 10.2 %collective-permute-start.2 = (bf16[15,1536]{0,1:T(8,128)(2,1)}, bf16[15,1536]{0,1:T(8,128)(2,1)}, u32[]{:S(2)}, u32[]{:S(2)}) collective-permute-start(bf16[15,1536]{0,1:T(8,128)(2,1)} %get-tuple-element.291), channel_id=1, source_target_pairs={{0,1},{1,2},{2,3},{3,4},{4,5},{5,6},{6,7},{7,8},{8,9},{9,10},{10,1... | collective-permute-start | bytes 138248 | tf_op jit(solution)/shard_map/ppermute | solution.py:28
  58.3 9.4 %collective-permute-start.3 = (bf16[15,1536]{0,1:T(8,128)(2,1)}, bf16[15,1536]{0,1:T(8,128)(2,1)}, u32[]{:S(2)}, u32[]{:S(2)}) collective-permute-start(bf16[15,1536]{0,1:T(8,128)(2,1)} %get-tuple-element.292), channel_id=1, source_target_pairs={{1,0},{2,1},{3,2},{4,3},{5,4},{6,5},{7,6},{8,7},{9,8},{10,9},{11,1... | collective-permute-start | bytes 138248 | tf_op jit(solution)/shard_map/ppermute | solution.py:30
  63.7 5.6 %copy-start.7 = (f32[1536]{0:T(1024)S(1)}, f32[1536]{0:T(1024)}, u32[]{:S(2)}) copy-start(f32[1536]{0:T(1024)} %get-tuple-element.199) | copy-start | bytes 18436
  63.7 5.6 %copy-start.8 = (f32[1536]{0:T(1024)S(1)}, f32[1536]{0:T(1024)}, u32[]{:S(2)}) copy-start(f32[1536]{0:T(1024)} %get-tuple-element.200) | copy-start | bytes 18436
  63.7 5.6 %copy-start.9 = (f32[1536]{0:T(1024)S(1)}, f32[1536]{0:T(1024)}, u32[]{:S(2)}) copy-start(f32[1536]{0:T(1024)} %get-tuple-element.201) | copy-start | bytes 18436
  63.7 5.6 %copy-start.10 = (f32[1536]{0:T(1024)S(1)}, f32[1536]{0:T(1024)}, u32[]{:S(2)}) copy-start(f32[1536]{0:T(1024)} %get-tuple-element.202) | copy-start | bytes 18436
  63.7 5.6 %copy-start.11 = (f32[1536]{0:T(1024)S(1)}, f32[1536]{0:T(1024)}, u32[]{:S(2)}) copy-start(f32[1536]{0:T(1024)} %get-tuple-element.203) | copy-start | bytes 18436
  63.7 5.6 %copy-start.12 = (f32[1536]{0:T(1024)S(1)}, f32[1536]{0:T(1024)}, u32[]{:S(2)}) copy-start(f32[1536]{0:T(1024)} %get-tuple-element.204) | copy-start | bytes 18436
  63.7 5.6 %copy-start.13 = (f32[1536]{0:T(1024)S(1)}, f32[1536]{0:T(1024)}, u32[]{:S(2)}) copy-start(f32[1536]{0:T(1024)} %get-tuple-element.205) | copy-start | bytes 18436
  63.8 5.6 %copy-start.14 = (f32[1536]{0:T(1024)S(1)}, f32[1536]{0:T(1024)}, u32[]{:S(2)}) copy-start(f32[1536]{0:T(1024)} %get-tuple-element.206) | copy-start | bytes 18436
  96.6 6.2 %copy-start.54 = (pred[128]{0:T(512)(128)(4,1)S(1)}, pred[128]{0:T(512)(128)(4,1)}, u32[]{:S(2)}) copy-start(pred[128]{0:T(512)(128)(4,1)} %get-tuple-element.297) | copy-start | bytes 388
  96.6 6.2 %copy-start.55 = (pred[128]{0:T(512)(128)(4,1)S(1)}, pred[128]{0:T(512)(128)(4,1)}, u32[]{:S(2)}) copy-start(pred[128]{0:T(512)(128)(4,1)} %get-tuple-element.298) | copy-start | bytes 388
  96.6 6.2 %copy-start.56 = (pred[128]{0:T(512)(128)(4,1)S(1)}, pred[128]{0:T(512)(128)(4,1)}, u32[]{:S(2)}) copy-start(pred[128]{0:T(512)(128)(4,1)} %get-tuple-element.299) | copy-start | bytes 388
  97.5 32.0 %collective-permute-start.4 = (bf16[15,1536]{0,1:T(8,128)(2,1)}, bf16[15,1536]{0,1:T(8,128)(2,1)}, u32[]{:S(2)}, u32[]{:S(2)}) collective-permute-start(bf16[15,1536]{0,1:T(8,128)(2,1)} %get-tuple-element.289), channel_id=1, source_target_pairs={{0,1},{1,2},{2,3},{3,4},{4,5},{5,6},{6,7},{7,8},{8,9},{9,10},{10,1... | collective-permute-start | bytes 138248 | tf_op jit(solution)/shard_map/ppermute | solution.py:28
  99.4 30.1 %collective-permute-start.5 = (bf16[15,1536]{0,1:T(8,128)(2,1)S(1)}, bf16[15,1536]{0,1:T(8,128)(2,1)}, u32[]{:S(2)}, u32[]{:S(2)}) collective-permute-start(bf16[15,1536]{0,1:T(8,128)(2,1)S(1)} %get-tuple-element.290), channel_id=1, source_target_pairs={{1,0},{2,1},{3,2},{4,3},{5,4},{6,5},{7,6},{8,7},{9,8},{10,9},{11,1... | collective-permute-start | bytes 138248 | tf_op jit(solution)/shard_map/ppermute | solution.py:30
  131.1 19.2 %copy-start.6 = (f32[1536]{0:T(1024)S(1)}, f32[1536]{0:T(1024)}, u32[]{:S(2)}) copy-start(f32[1536]{0:T(1024)} %param.16) | copy-start | bytes 18436
  131.1 19.2 %copy-start.58 = (f32[128]{0:T(128)S(1)}, f32[128]{0:T(128)}, u32[]{:S(2)}) copy-start(f32[128]{0:T(128)} %copy-done.57) | copy-start | bytes 1540
  131.1 19.2 %copy-start.60 = (f32[128]{0:T(128)S(1)}, f32[128]{0:T(128)}, u32[]{:S(2)}) copy-start(f32[128]{0:T(128)} %copy-done.59) | copy-start | bytes 1540
  199.4 6.8 %copy-start.1 = (f32[128,1536]{0,1:T(8,128)S(1)}, f32[128,1536]{0,1:T(8,128)}, u32[]{:S(2)}) copy-start(f32[128,1536]{0,1:T(8,128)} %get-tuple-element.273) | copy-start | bytes 2359300
  200.9 6.5 %copy-start.38 = (f32[1536]{0:T(1024)S(1)}, f32[1536]{0:T(1024)}, u32[]{:S(2)}) copy-start(f32[1536]{0:T(1024)} %get-tuple-element.198) | copy-start | bytes 18436
  200.9 6.5 %copy-start.39 = (f32[1536]{0:T(1024)S(1)}, f32[1536]{0:T(1024)}, u32[]{:S(2)}) copy-start(f32[1536]{0:T(1024)} %get-tuple-element.195) | copy-start | bytes 18436
  200.9 207.0 %collective-permute-start.6 = (bf16[128,2,1536]{0,2,1:T(8,128)(2,1)}, bf16[128,2,1536]{0,2,1:T(8,128)(2,1)}, u32[]{:S(2)}, u32[]{:S(2)}) collective-permute-start(bf16[128,2,1536]{0,2,1:T(8,128)(2,1)} %get-tuple-element.283), channel_id=1, source_target_pairs={{0,1},{1,2},{2,3},{3,4},{4,5},{5,6},{6,7},{7,8},{8,9},{9,10},{10,1... | collective-permute-start | bytes 2359304 | tf_op jit(solution)/shard_map/ppermute | solution.py:17
  203.5 204.5 %collective-permute-start.7 = (bf16[128,2,1536]{0,2,1:T(8,128)(2,1)}, bf16[128,2,1536]{0,2,1:T(8,128)(2,1)}, u32[]{:S(2)}, u32[]{:S(2)}) collective-permute-start(bf16[128,2,1536]{0,2,1:T(8,128)(2,1)} %get-tuple-element.284), channel_id=1, source_target_pairs={{1,0},{2,1},{3,2},{4,3},{5,4},{6,5},{7,6},{8,7},{9,8},{10,9},{11,1... | collective-permute-start | bytes 2359304 | tf_op jit(solution)/shard_map/ppermute | solution.py:17
  (38 other events, 201.8 us)
Sparse Core Ops, SparseCore 0:
  129.6 276.6 all-reduce.3
where the time goes:
time: 421 us; the launch traced here: 419 us
  blocking collectives  113 us (27%)
  waiting for transfers between devices  89.3 us (21%)
  other arithmetic  70.2 us (17%)
  matrix products  55.7 us (13%)
  local copies, waits for them, and re-layouts  46.8 us (11%)
  starting transfers between devices  27.8 us (7%)
  between operations  15.1 us (4%)
    psum x1, blocking collectives, per_device(): lax.psum((gain_part, kernel_part, bias_part), ('dp', 'seq'))  113 us
    psum x1, waiting for transfers between devices, per_device(): lax.psum((gain_part, kernel_part, bias_part), ('dp', 'seq'))  83.9 us
    reduce_sum x4, other arithmetic, per_device(): jnp.sum(jnp.where(same_taps[tap_index], conv_wide[tap_index:tap_index + f...  29 us
    another operation x32, local copies, waits for them, and re-layouts, per_device(): kernel_part = jnp.stack(kernel_rows, 0)  24.4 us
    reduce_sum x1, other arithmetic, per_device(): gain_part = jnp.sum(grad_in * normed, 0)  19.2 us
    ppermute x4, starting transfers between devices, shifted(): return lax.ppermute(block, axis, route)  16 us
    dot_general x12, matrix products, masked_logits(): jnp.einsum('qhe,khe->hqk', query_rows, key_rows, preferred_element_type=j...  15.4 us
    dot_general x6, matrix products, backward_group(): jnp.einsum('hqk,qhe->khe', grad_logit, query_rows, preferred_element_type...  10.9 us
  transfers between devices with their start and end apart: 9, of which 3 were waited for; matrix products, arithmetic and copies ran while one was open for 27% of the time, Pallas kernels for 0%

commit v1 on v0

--- a/solution.py
+++ b/solution.py
@@ -211,7 +211,9 @@
     key_grad = own_grad[:, 0]
     value_grad = own_grad[:, 1]
     query_grad = from_groups(query_blocks)
-    gain_sum, kernel_sum, bias_sum = lax.psum((gain_part, kernel_part, bias_part), ("dp", "seq"))
+    gain_sum, kernel_sum, bias_sum = lax.psum(
+        lax.psum((gain_part, kernel_part, bias_part), "seq"), "dp"
+    )
     norm_factor = (lax.axis_size("dp") * lax.axis_size("seq") * frame_count) ** (-0.5)
     return (
         conv_out[None],

time: 421 us -> 588 us (1.40)
  blocking collectives: 113 us -> 270 us
  waiting for transfers between devices: 89.3 us -> 101 us
    psum x1 -> x2, blocking collectives: 113 us -> 270 us  [the longest x1 247 us: per_device(): lax.psum((gain_part, kernel_part, bias_part), 'seq')]
    psum x1 -> x2, waiting for transfers between devices: 83.9 us -> 92.6 us  [the longest x1 92.6 us: per_device(): lax.psum(lax.psum((gain_part, kernel_part, bias_part), 'seq'), 'dp')]
  transfers between devices with their start and end apart: 9 -> 10, of which waited for: 3 -> 4; matrix products, arithmetic and copies ran while one was open for 27% -> 18% of each run, Pallas kernels for 0% -> 0%
where the time goes in v1:
time: 588 us; the launch traced here: 582 us
  blocking collectives  270 us (46%)
  waiting for transfers between devices  101 us (17%)
  other arithmetic  69.3 us (12%)
  matrix products  50.6 us (9%)
  local copies, waits for them, and re-layouts  47 us (8%)
  starting transfers between devices  27.9 us (5%)
  between operations  15.6 us (3%)
    psum x1, blocking collectives, per_device(): lax.psum((gain_part, kernel_part, bias_part), 'seq')  247 us
    psum x1, waiting for transfers between devices, per_device(): lax.psum(lax.psum((gain_part, kernel_part, bias_part), 'seq'), 'dp')  92.6 us
    reduce_sum x4, other arithmetic, per_device(): jnp.sum(jnp.where(same_taps[tap_index], conv_wide[tap_index:tap_index + f...  29.1 us
    another operation x32, local copies, waits for them, and re-layouts, per_device(): kernel_part = jnp.stack(kernel_rows, 0)  24.4 us
    psum x1, blocking collectives, per_device(): lax.psum(lax.psum((gain_part, kernel_part, bias_part), 'seq'), 'dp')  23.4 us
    reduce_sum x1, other arithmetic, per_device(): gain_part = jnp.sum(grad_in * normed, 0)  16.9 us
    ppermute x4, starting transfers between devices, shifted(): return lax.ppermute(block, axis, route)  16 us
  transfers between devices with their start and end apart: 10, of which 4 were waited for; matrix products, arithmetic and copies ran while one was open for 18% of the time, Pallas kernels for 0%

profile of v1, /device:TPU:1, one launch (start us, length us, event | category | flops | bytes accessed | tf_op | source)
XLA Modules:
  0.0 581.6 jit_solution(11939641245212514185)
XLA Ops:
  8.5 8.7 %collective-permute-start.1 = (bf16[128,2,1536]{2,0,1:T(8,128)(2,1)S(1)}, bf16[128,2,1536]{2,0,1:T(8,128)(2,1)S(1)}, u32[]{:S(2)}, u32[]{:S(2)}) collective-permute-start(bf16[128,2,1536]{2,0,1:T(8,128)(2,1)S(1)} %pad_maximum_fusion.2), channel_id=1, source_target_pairs={{1,0},{2,1},{3,2},{4,3},{5,4},{6,5},{7,6},{8,7},{9,8},{10,9},{11,1... | collective-permute-start | bytes 2359304 | tf_op jit(solution)/shard_map/ppermute | solution.py:17
  17.3 1.9 collective-permute-start
  23.6 4.5 collective-permute-done
  31.3 1.8 copy.25
  34.6 16.4 %while.28 = (s32[]{:T(128)}, bf16[6,128,4,64]{1,3,2,0:T(8,128)(2,1)S(1)}, f32[6,4,128]{2,1,0:T(4,128)}, bf16[6,384,4,64]{1,3,2,0:T(8,128)(2,1)}, bf16[6,128,4,64...) while((s32[]{:T(128)}, ...), condition=%wide.region_3.4_spmd.clone, body=%wide.region_0.3_spmd.clone.sunk | while | flops 51953152 | bytes 3068009 | solution.py:115
  53.0 4.5 collective-permute-start.2
  57.5 2.1 collective-permute-start.3
  59.6 2.2 slice_reduce_fusion.29
  63.4 3.5 collective-permute-done.3
  68.8 18.7 %fusion.110 = (f32[1536]{0:T(1024)S(1)}, f32[1536]{0:T(1024)S(1)}, f32[1536]{0:T(1024)S(1)}, f32[1536]{0:T(1024)S(1)}, f32[1536]{0:T(1024)S(1)}, /*index=5*/f32[...) fusion(f32[158,1536]{0,1:T(8,128)S(1)} %maximum_convert_fusion,, ...), kind=kLoop, calls=%fused_computation.158 | loop fusion | flops 25741824 | bytes 26208128 | tf_op jit(solution)/shard_map/reduce_sum | solution.py:143
  87.6 4.4 fusion.112
  92.1 3.7 fusion.114
  96.8 1.9 collective-permute-start.4
  98.7 3.4 collective-permute-start.5
  102.1 2.2 fusion.108
  122.8 6.0 %stack.135 = f32[31,1536]{1,0:T(8,128)} concatenate(f32[1,1536]{1,0:T(1,128)} %stack.104, f32[1,1536]{1,0:T(1,128)} %stack.105, f32[1,1536]{1,0:T(1,128)} %stack.106, f32[1,1536]{1,0:T(1,128)} %stack.107, f32[1,1536]{1,0:T(1,128)} %stack.108, f32[1,1536]{1,0:T(1,128)} %stack.109, f32[1,1536]{1,0:T(1,128)} %stack.110, f32[1,1536]{1,0:T(1,128)} %stack.111, f32[1,1536]{1,0:T(1,128)} %stack.112, ...), dimensions={0} | concatenate | bytes 380928 | tf_op jit(solution)/shard_map/stack | solution.py:152
  131.1 16.9 %fusion.190 = (f32[1536]{0:T(1024)}, f32[128]{0:T(128)S(1)}, f32[128]{0:T(128)S(1)}, f32[128,1536]{0,1:T(8,128)S(1)}) fusion(bf16[6,128,4,64]{1,3,2,0:T(8,128)(2,1)S(1)} %get-tuple-element.104, f32[128]{0:T(128)} %copy-done.95, f32[128]{0:T(128)} %copy-done.93, f32[1536]{0:T(1024)S(1)} %copy-done.10, f32[158,1536]{0,1:T(8,128)S(1)} %maximum_convert_fusion.1, ...), kind=kLoop, calls=%fused_computation.277 | loop fusion | flops 19855616 | bytes 25767808 | tf_op jit(solution)/shard_map/reduce_sum | solution.py:160
  149.8 45.2 %while.29 = (s32[]{:T(128)}, bf16[6,128,4,64]{1,3,2,0:T(8,128)(2,1)S(1)}, f32[6,384,4,64]{1,3,2,0:T(8,128)}, f32[6,384,4,64]{1,3,2,0:T(8,128)S(1)}, bf16[6,384,4...) while((s32[]{:T(128)}, ...), condition=%wide.region_10.11_spmd.clone, body=%wide.region_9.10_spmd.clone.sunk | while | flops 127451136 | bytes 5426313 | solution.py:192
  155.5 1.8 fusion.240
  163.0 1.8 fusion.240
  170.6 1.8 fusion.240
  178.1 1.8 fusion.240
  185.7 1.8 fusion.240
  193.2 1.8 fusion.240
  195.0 2.0 fusion.48
  198.5 2.5 collective-permute-start.6
  201.1 2.8 collective-permute-start.7
  205.9 246.7 %all-reduce.1 = (f32[1536]{0:T(1024)S(1)}, f32[1536]{0:T(1024)S(1)}) all-reduce(f32[1536]{0:T(1024)S(1)} %copy-done.74, f32[1536]{0:T(1024)S(1)} %copy-done.73), channel_id=1, replica_groups=mesh['dp'=8,'seq'=64] {'seq'}, use_global_device_ids=true, to_apply=%region_12.13 | all-reduce | flops 3072 | bytes 24576 | tf_op jit(solution)/shard_map/psum | solution.py:215
  452.7 23.4 %all-reduce.2 = (f32[1536]{0:T(1024)S(1)}, f32[1536]{0:T(1024)S(1)}) all-reduce(f32[1536]{0:T(1024)S(1)} %get-tuple-element.270, f32[1536]{0:T(1024)S(1)} %get-tuple-element.271), channel_id=1, replica_groups=mesh['dp'=8,'seq'=64] {'dp'}, use_global_device_ids=true, to_apply=%region_13.14 | all-reduce | flops 3072 | bytes 24576 | tf_op jit(solution)/shard_map/psum | solution.py:214
  476.7 92.6 %all-reduce.8.cloned.1.call-done = f32[31,1536]{1,0:T(8,128)} async-done(((f32[31,1536]{1,0:T(8,128)}), f32[31,1536]{1,0:T(8,128)}) %all-reduce.8.cloned.1.call-update) | async-done | bytes 190480 | tf_op jit(solution)/shard_map/psum | solution.py:214
  569.4 1.6 broadcast_multiply_fusion
  571.0 1.9 fusion.52
  (339 shorter events, 94.8 us)
Async XLA Ops:
  7.2 21.0 %copy-start.4 = (bf16[1,128,1536]{2,1,0:T(8,128)(2,1)S(1)}, bf16[1,128,1536]{2,1,0:T(8,128)(2,1)}, u32[]{:S(2)}) copy-start(bf16[1,128,1536]{2,1,0:T(8,128)(2,1)} %param.14) | copy-start | bytes 1179652
  7.2 21.0 %copy-start.5 = (bf16[1,128,1536]{2,1,0:T(8,128)(2,1)S(1)}, bf16[1,128,1536]{2,1,0:T(8,128)(2,1)}, u32[]{:S(2)}) copy-start(bf16[1,128,1536]{2,1,0:T(8,128)(2,1)} %param.13) | copy-start | bytes 1179652
  7.2 12.1 %copy-start.8 = (f32[31,1536]{1,0:T(8,128)S(1)}, f32[31,1536]{1,0:T(8,128)}, u32[]{:S(2)}) copy-start(f32[31,1536]{1,0:T(8,128)} %param.17) | copy-start | bytes 571396
  7.2 13.0 %copy-start.9 = (s32[1,8192]{1,0:T(1,128)S(1)}, s32[1,8192]{1,0:T(1,128)}, u32[]{:S(2)}) copy-start(s32[1,8192]{1,0:T(1,128)} %param.15) | copy-start | bytes 98308
  7.2 13.0 %copy-start.7 = (bf16[1,128,1536]{2,1,0:T(8,128)(2,1)S(1)}, bf16[1,128,1536]{2,1,0:T(8,128)(2,1)}, u32[]{:S(2)}) copy-start(bf16[1,128,1536]{2,1,0:T(8,128)(2,1)} %param.12) | copy-start | bytes 1179652
  7.2 468.9 %all-reduce.6.cloned.1.call-start = ((), (), s32[]{:S(2)}) async-start(), calls=%async_computation | async-start | bytes 393216 | tf_op jit(solution)/shard_map/psum | solution.py:215
  8.5 14.2 %collective-permute-start.1 = (bf16[128,2,1536]{2,0,1:T(8,128)(2,1)S(1)}, bf16[128,2,1536]{2,0,1:T(8,128)(2,1)S(1)}, u32[]{:S(2)}, u32[]{:S(2)}) collective-permute-start(bf16[128,2,1536]{2,0,1:T(8,128)(2,1)S(1)} %pad_maximum_fusion.2), channel_id=1, source_target_pairs={{1,0},{2,1},{3,2},{4,3},{5,4},{6,5},{7,6},{8,7},{9,8},{10,9},{11,1... | collective-permute-start | bytes 2359304 | tf_op jit(solution)/shard_map/ppermute | solution.py:17
  17.3 10.8 %collective-permute-start = (bf16[128,2,1536]{2,0,1:T(8,128)(2,1)S(1)}, bf16[128,2,1536]{2,0,1:T(8,128)(2,1)}, u32[]{:S(2)}, u32[]{:S(2)}) collective-permute-start(bf16[128,2,1536]{2,0,1:T(8,128)(2,1)S(1)} %pad_maximum_fusion.2), channel_id=1, source_target_pairs={{0,1},{1,2},{2,3},{3,4},{4,5},{5,6},{6,7},{7,8},{8,9},{9,10},{10,1... | collective-permute-start | bytes 2359304 | tf_op jit(solution)/shard_map/ppermute | solution.py:17
  34.6 17.1 %copy-start.10 = (f32[1536]{0:T(1024)S(1)}, f32[1536]{0:T(1024)}, u32[]{:S(2)}) copy-start(f32[1536]{0:T(1024)} %param.16) | copy-start | bytes 18436
  51.2 10.6 %copy-start.93 = (f32[128]{0:T(128)}, f32[128]{0:T(128)S(1)}, u32[]{:S(2)}) copy-start(f32[128]{0:T(128)S(1)} %broadcast_multiply_fusion.5) | copy-start | bytes 1540
  51.7 10.1 %copy-start.95 = (f32[128]{0:T(128)}, f32[128]{0:T(128)S(1)}, u32[]{:S(2)}) copy-start(f32[128]{0:T(128)S(1)} %add_rsqrt_fusion) | copy-start | bytes 1540
  53.0 10.4 %collective-permute-start.2 = (bf16[15,1536]{0,1:T(8,128)(2,1)}, bf16[15,1536]{0,1:T(8,128)(2,1)}, u32[]{:S(2)}, u32[]{:S(2)}) collective-permute-start(bf16[15,1536]{0,1:T(8,128)(2,1)} %get-tuple-element.293), channel_id=1, source_target_pairs={{0,1},{1,2},{2,3},{3,4},{4,5},{5,6},{6,7},{7,8},{8,9},{9,10},{10,1... | collective-permute-start | bytes 138248 | tf_op jit(solution)/shard_map/ppermute | solution.py:28
  57.5 9.4 %collective-permute-start.3 = (bf16[15,1536]{0,1:T(8,128)(2,1)}, bf16[15,1536]{0,1:T(8,128)(2,1)}, u32[]{:S(2)}, u32[]{:S(2)}) collective-permute-start(bf16[15,1536]{0,1:T(8,128)(2,1)} %get-tuple-element.294), channel_id=1, source_target_pairs={{1,0},{2,1},{3,2},{4,3},{5,4},{6,5},{7,6},{8,7},{9,8},{10,9},{11,1... | collective-permute-start | bytes 138248 | tf_op jit(solution)/shard_map/ppermute | solution.py:30
  63.0 5.5 copy-start.11
  63.0 5.5 copy-start.13
  63.0 5.5 copy-start.15
  63.0 5.5 copy-start.17
  63.0 5.5 copy-start.19
  63.0 5.5 copy-start.21
  95.8 6.2 %copy-start.90 = (pred[128]{0:T(512)(128)(4,1)S(1)}, pred[128]{0:T(512)(128)(4,1)}, u32[]{:S(2)}) copy-start(pred[128]{0:T(512)(128)(4,1)} %get-tuple-element.299) | copy-start | bytes 388
  95.8 6.2 %copy-start.91 = (pred[128]{0:T(512)(128)(4,1)S(1)}, pred[128]{0:T(512)(128)(4,1)}, u32[]{:S(2)}) copy-start(pred[128]{0:T(512)(128)(4,1)} %get-tuple-element.300) | copy-start | bytes 388
  95.8 6.2 %copy-start.92 = (pred[128]{0:T(512)(128)(4,1)S(1)}, pred[128]{0:T(512)(128)(4,1)}, u32[]{:S(2)}) copy-start(pred[128]{0:T(512)(128)(4,1)} %get-tuple-element.301) | copy-start | bytes 388
  96.8 32.4 %collective-permute-start.4 = (bf16[15,1536]{0,1:T(8,128)(2,1)}, bf16[15,1536]{0,1:T(8,128)(2,1)}, u32[]{:S(2)}, u32[]{:S(2)}) collective-permute-start(bf16[15,1536]{0,1:T(8,128)(2,1)} %get-tuple-element.291), channel_id=1, source_target_pairs={{0,1},{1,2},{2,3},{3,4},{4,5},{5,6},{6,7},{7,8},{8,9},{9,10},{10,1... | collective-permute-start | bytes 138248 | tf_op jit(solution)/shard_map/ppermute | solution.py:28
  98.7 30.5 %collective-permute-start.5 = (bf16[15,1536]{0,1:T(8,128)(2,1)S(1)}, bf16[15,1536]{0,1:T(8,128)(2,1)}, u32[]{:S(2)}, u32[]{:S(2)}) collective-permute-start(bf16[15,1536]{0,1:T(8,128)(2,1)S(1)} %get-tuple-element.292), channel_id=1, source_target_pairs={{1,0},{2,1},{3,2},{4,3},{5,4},{6,5},{7,6},{8,7},{9,8},{10,9},{11,1... | collective-permute-start | bytes 138248 | tf_op jit(solution)/shard_map/ppermute | solution.py:30
  128.8 440.6 %all-reduce.8.cloned.1.call-start = ((), (), s32[]{:S(2)}) async-start(), calls=%async_computation.1 | async-start | bytes 393216 | tf_op jit(solution)/shard_map/psum | solution.py:214
  131.0 16.9 %copy-start.94 = (f32[128]{0:T(128)S(1)}, f32[128]{0:T(128)}, u32[]{:S(2)}) copy-start(f32[128]{0:T(128)} %copy-done.93) | copy-start | bytes 1540
  131.0 16.9 %copy-start.96 = (f32[128]{0:T(128)S(1)}, f32[128]{0:T(128)}, u32[]{:S(2)}) copy-start(f32[128]{0:T(128)} %copy-done.95) | copy-start | bytes 1540
  197.0 6.8 %copy-start.2 = (f32[128,1536]{0,1:T(8,128)S(1)}, f32[128,1536]{0,1:T(8,128)}, u32[]{:S(2)}) copy-start(f32[128,1536]{0,1:T(8,128)} %get-tuple-element.275) | copy-start | bytes 2359300
  198.5 7.4 %copy-start.73 = (f32[1536]{0:T(1024)S(1)}, f32[1536]{0:T(1024)}, u32[]{:S(2)}) copy-start(f32[1536]{0:T(1024)} %get-tuple-element.198) | copy-start | bytes 18436
  198.5 7.4 %copy-start.74 = (f32[1536]{0:T(1024)S(1)}, f32[1536]{0:T(1024)}, u32[]{:S(2)}) copy-start(f32[1536]{0:T(1024)} %get-tuple-element.195) | copy-start | bytes 18436
  198.5 372.5 %collective-permute-start.6 = (bf16[128,2,1536]{0,2,1:T(8,128)(2,1)}, bf16[128,2,1536]{0,2,1:T(8,128)(2,1)}, u32[]{:S(2)}, u32[]{:S(2)}) collective-permute-start(bf16[128,2,1536]{0,2,1:T(8,128)(2,1)} %get-tuple-element.285), channel_id=1, source_target_pairs={{0,1},{1,2},{2,3},{3,4},{4,5},{5,6},{6,7},{7,8},{8,9},{9,10},{10,1... | collective-permute-start | bytes 2359304 | tf_op jit(solution)/shard_map/ppermute | solution.py:17
  201.1 369.9 %collective-permute-start.7 = (bf16[128,2,1536]{0,2,1:T(8,128)(2,1)}, bf16[128,2,1536]{0,2,1:T(8,128)(2,1)}, u32[]{:S(2)}, u32[]{:S(2)}) collective-permute-start(bf16[128,2,1536]{0,2,1:T(8,128)(2,1)} %get-tuple-element.286), channel_id=1, source_target_pairs={{1,0},{2,1},{3,2},{4,3},{5,4},{6,5},{7,6},{8,7},{9,8},{10,9},{11,1... | collective-permute-start | bytes 2359304 | tf_op jit(solution)/shard_map/ppermute | solution.py:17
  (75 other events, 277.9 us)
Sparse Core Ops, SparseCore 0:
  128.9 200.1 all-reduce.5
  476.3 93.0 all-reduce.7
